TPU v7x, 32 devices: a whole 2x2x4 slice. The times are simulated.
32 devices in a mesh: grp: 2 (over y), ctx: 4 (over z), chan: 4 (over x, core).
Axes of the slice: x: 2, y: 2, z: 4, core: 2. Of those that a mesh axis runs over, the one named last changes fastest.
Arguments:
- grad_out: bfloat16 [1024, 4096], P(('grp', 'ctx'), 'chan'), parts along dimension 0, may hold values from -6 to 6
- gate_act: bfloat16 [1024, 4096], P(('grp', 'ctx'), 'chan'), parts along dimension 0, may hold values from -6 to 6
- conv_input: bfloat16 [1024, 4096], P(('grp', 'ctx'), 'chan'), parts along dimension 0, may hold values from -0.26367188 to 0.26367188
- filter_taps: bfloat16 [512, 4096], P('ctx', 'chan'), may hold values from -0.26367188 to 0.26367188
- skip_gain: float32 [4096], P('chan'), may hold values from -4 to 4
Outputs:
- grad_input: bfloat16 [1024, 4096], P(('grp', 'ctx'), 'chan'), parts along dimension 0
- grad_filter: float32 [1024, 4096], P(('grp', 'ctx'), 'chan'), parts along dimension 0
There are 2 independent parts, one for each index of `grp`. A program takes and returns all parts, laid end to end along the dimension named above; an argument that names none is the same for every part. Nothing has to cross between parts.
All inputs are finite; a program needn't handle non-finite values.
Results may differ from a plain program's by a relative error of at most 0.014.
Values may be sent and summed in bfloat16 or wider, within the bound.
No kernel may reach another device: no remote copies, remote signals or barrier semaphores. Data moves between devices by JAX's collectives and lax.ppermute only.
A program may use at most 64 MiB of HBM per device.

v0:
```python
import jax
import jax.numpy as jnp
from jax import lax
from jax.sharding import PartitionSpec as P


def split_parts(values):
    high_part = values.astype(jnp.bfloat16)
    low_part = (values - high_part.astype(jnp.float32)).astype(jnp.bfloat16)
    return (high_part, low_part)


def phase_tables(row_count, col_count, shift, period):
    row_index = jnp.arange(row_count, dtype=jnp.int32)[:, None] + shift
    col_index = jnp.arange(col_count, dtype=jnp.int32)[None, :]
    angles = (row_index * col_index % period).astype(jnp.float32) * (2.0 * jnp.pi / period)
    return (split_parts(jnp.cos(angles)), split_parts(jnp.sin(angles)))


def table_times(table, signal):
    high_part, low_part = table
    return jnp.dot(high_part, signal, preferred_element_type=jnp.float32) + jnp.dot(
        low_part, signal, preferred_element_type=jnp.float32
    )


def table_times_float(table, values):
    high_part, low_part = table
    value_high, value_low = split_parts(values)
    total = jnp.dot(high_part, value_high, preferred_element_type=jnp.float32)
    total = total + jnp.dot(high_part, value_low, preferred_element_type=jnp.float32)
    return total + jnp.dot(low_part, value_high, preferred_element_type=jnp.float32)


def forward_spectra(tables, signal):
    cos_part, sin_part = tables
    return (table_times(cos_part, signal), -table_times(sin_part, signal))


def inverse_spectra(tables, spectra, period):
    cos_part, sin_part = tables
    return (
        table_times_float(cos_part, spectra[0]) - table_times_float(sin_part, spectra[1])
    ) / period


def batched_times(table, blocks):
    high_part, low_part = table
    return jnp.einsum(
        "pr,nrc->npc", high_part, blocks, preferred_element_type=jnp.float32
    ) + jnp.einsum("pr,nrc->npc", low_part, blocks, preferred_element_type=jnp.float32)


def times_conj(first_spec, second_spec):
    return (
        first_spec[0] * second_spec[0] + first_spec[1] * second_spec[1],
        first_spec[1] * second_spec[0] - first_spec[0] * second_spec[1],
    )


def shards(grad_out, gate_act, conv_input, filter_taps, skip_gain):
    span_len = grad_out.shape[0]
    channels = grad_out.shape[1]
    period = 2 * span_len
    cycle_size = lax.axis_size("ctx")
    own_index = lax.axis_index("ctx")
    grad_y = (grad_out.astype(jnp.float32) * gate_act.astype(jnp.float32)).astype(jnp.bfloat16)
    short_fwd = phase_tables(period, span_len, 0, period)
    full_fwd = phase_tables(period, period, 0, period)
    short_inv = phase_tables(span_len, period, span_len, period)
    full_inv = phase_tables(period, period, span_len, period)
    taps = lax.all_gather(filter_taps, "ctx", axis=0, tiled=True)
    taps_padded = jnp.concatenate([jnp.zeros((span_len, channels), jnp.bfloat16), taps], axis=0)
    windows = jnp.concatenate(
        [
            taps_padded[:-span_len].reshape(cycle_size, span_len, channels),
            taps_padded[span_len:].reshape(cycle_size, span_len, channels),
        ],
        axis=1,
    )
    window_real = batched_times(full_fwd[0], windows)
    window_imag = -batched_times(full_fwd[1], windows)
    own_input_spec = forward_spectra(short_fwd, conv_input)
    zero_spec = jnp.zeros((period, channels), jnp.float32)
    lag_sums = jnp.zeros((taps_padded.shape[0], channels), jnp.float32)

    def add_pair(lag_totals, grad_spec, input_spec, distance):
        window_spec = (
            lax.dynamic_index_in_dim(window_real, distance, 0, keepdims=False),
            lax.dynamic_index_in_dim(window_imag, distance, 0, keepdims=False),
        )
        product = times_conj(grad_spec, window_spec)
        start_row = distance * span_len
        lag_window = inverse_spectra(full_inv, times_conj(grad_spec, input_spec), period)
        current = lax.dynamic_slice_in_dim(lag_totals, start_row, period, 0)
        lag_totals = lax.dynamic_update_slice_in_dim(lag_totals, current + lag_window, start_row, 0)
        return (product, lag_totals)

    spans = lax.all_gather(grad_y[None], "ctx", axis=0, tiled=True)

    def span_step(offset, current):
        distance = offset - own_index

        def run_pair(values_now):
            arrived = lax.dynamic_index_in_dim(spans, offset, 0, keepdims=False)
            product, new_sums = add_pair(
                values_now[2], forward_spectra(short_fwd, arrived), own_input_spec, distance
            )
            return (values_now[0] + product[0], values_now[1] + product[1], new_sums)

        return lax.cond(distance >= 0, run_pair, lambda values_now: values_now, current)

    home_real, home_imag, lag_sums = lax.fori_loop(
        0, spans.shape[0], span_step, (zero_spec, zero_spec, lag_sums)
    )
    conv_part = inverse_spectra(short_inv, (home_real, home_imag), period)
    grad_input = (conv_part + skip_gain[None, :] * grad_y.astype(jnp.float32)).astype(jnp.bfloat16)
    grad_filter = lax.psum_scatter(
        lag_sums[span_len:].astype(jnp.bfloat16), "ctx", scatter_dimension=0, tiled=True
    ).astype(jnp.float32)
    return (grad_input, grad_filter)


def solution(mesh):
    return jax.shard_map(
        shards,
        mesh=mesh,
        in_specs=(
            P(("grp", "ctx"), "chan"),
            P(("grp", "ctx"), "chan"),
            P(("grp", "ctx"), "chan"),
            P("ctx", "chan"),
            P("chan"),
        ),
        out_specs=(P(("grp", "ctx"), "chan"), P(("grp", "ctx"), "chan")),
        check_vma=False,
    )
```

profile of v0, /device:TPU:0, one launch (start us, length us, event | category | flops | bytes accessed | tf_op | source)
XLA Modules:
  0.0 181.5 jit_solution(1788791915903343266)
XLA Ops:
  8.0 1.8 multiply_convert_fusion
  15.4 24.8 %all-gather.4.cloned.1.call-done = bf16[512,1024]{1,0:T(8,128)(2,1)} async-done(((bf16[128,1024]{1,0:T(8,128)(2,1)}), bf16[512,1024]{1,0:T(8,128)(2,1)}) %all-gather.4.cloned.1.call-update) | async-done | bytes 1048592 | tf_op jit(solution)/shard_map/all_gather | solution.py:72
  46.4 3.6 %add_bitcast_fusion = f32[4,256,1024]{1,2,0:T(8,128)} fusion(f32[4,1024,256]{2,1,0:T(8,128)S(1)} %fusion.93, bf16[4,128,1024]{1,2,0:T(8,128)(2,1)S(1)} %copy.11, bf16[4,128,1024]{1,2,0:T(8,128)(2,1)S(1)} %copy.10), kind=kOutput, calls=%fused_computation.87 | convolution fusion | flops 543293440 | bytes 10485760 | tf_op jit(solution)/shard_map/pr,nrc->npc/dot_general | solution.py:51
  50.0 3.7 %negate_bitcast_fusion = f32[4,256,1024]{1,2,0:T(8,128)} fusion(f32[4,1024,256]{2,1,0:T(8,128)S(1)} %fusion.91, bf16[4,128,1024]{1,2,0:T(8,128)(2,1)S(1)} %copy.11, bf16[4,128,1024]{1,2,0:T(8,128)(2,1)S(1)} %copy.10), kind=kOutput, calls=%fused_computation.86 | convolution fusion | flops 544342016 | bytes 10485760 | tf_op jit(solution)/shard_map/pr,nrc->npc/dot_general | solution.py:51
  53.7 16.3 %all-gather.6.cloned.1.call-done = bf16[512,1024]{1,0:T(8,128)(2,1)} async-done(((bf16[128,1024]{1,0:T(8,128)(2,1)}), bf16[512,1024]{1,0:T(8,128)(2,1)}) %all-gather.6.cloned.1.call-update) | async-done | bytes 1048592 | tf_op jit(solution)/shard_map/all_gather | solution.py:99
  70.0 1.7 broadcast_in_dim.7
  73.9 70.8 %while.20 = (s32[]{:T(128)}, f32[256,1024]{0,1:T(8,128)}, f32[256,1024]{0,1:T(8,128)}, f32[640,1024]{0,1:T(8,128)}, s32[]{:T(128)}, /*index=5*/bf16[4,128,1024]{...) while((s32[]{:T(128)}, f32[256,1024]{0,1:T(8,128)}, ...), condition=%wide.region_3.4_spmd.clone.clone.clone, body=%wide.region_0.3_spmd.clone.clone.clone.sunk | while | flops 1085865984 | bytes 40109640 | solution.py:113
  73.9 1.9 %subtract_convert_fusion.25 = (bf16[256,256]{1,0:T(8,128)(2,1)}, bf16[256,256]{1,0:T(8,128)(2,1)}, bf16[256,256]{1,0:T(8,128)(2,1)S(1)}, bf16[256,256]{1,0:T(8,128)(2,1)}) fusion(s32[256]{0:T(256)S(1)} %get-tuple-element.688), kind=kLoop, calls=%fused_computation.62.clone.1 | loop fusion | flops 1441792 | bytes 525312 | tf_op jit(solution)/shard_map/convert_element_type | solution.py:9
  78.1 13.5 %conditional.5 = ((f32[256,1024]{0,1:T(8,128)}, f32[256,1024]{0,1:T(8,128)}, f32[640,1024]{0,1:T(8,128)})) conditional(s32[]{:T(128)} %convert_element_type.670, (f32[256,1024]{0,1:T(8,128)}, f32[256,1024]{0,1:T(8,128)}, f32[640,1024]{0,1:T(8,128)}) %tuple.73, (s32[]{:T(128)}, bf16[4,128,1024]{2,1,0:T(8,128)(2,1)}, bf16[256,128]{1,0:T(8,128)(2,1)}, ...), branch_computations={%region_1.1_spmd, %region_2.2_spmd} | conditional | flops 1083179008 | bytes 39321852 | solution.py:111
  82.0 5.0 %multiply_subtract_fusion = (f32[256,1024]{0,1:T(8,128)S(1)}, f32[256,1024]{0,1:T(8,128)S(1)}, f32[256,1024]{0,1:T(8,128)}, f32[256,1024]{0,1:T(8,128)}) fusion(f32[256,1024]{0,1:T(8,128)} %get-tuple-element.336, f32[256,1024]{0,1:T(8,128)S(1)} %fusion.22, f32[256,1024]{0,1:T(8,128)} %get-tuple-element.335, f32[256,1024]{0,1:T(8,128)} %get-tuple-element.323, ...), kind=kOutput, calls=%fused_computation.31 | convolution fusion | flops 71041024 | bytes 12910600 | tf_op jit(solution)/shard_map/while/body/eval_jaxpr/cond/branch_1_fun/dot_general | solution.py:22
  88.9 2.7 %fusion.20 = f32[640,1024]{0,1:T(8,128)} fusion(f32[640,1024]{0,1:T(8,128)} %get-tuple-element.334, s32[]{:T(128)S(6)} %select_n.24, f32[1024,256]{1,0:T(8,128)S(1)} %convolution_add_fusion.2, f32[1024,256]{1,0:T(8,128)S(1)} %convolution_add_fusion.1, bf16[256,256]{1,0:T(8,128)(2,1)S(1)} %copy-done.2, f32[256,1024]{0,1:T(8,128)S(1)} %get-tuple-element.545), kind=kOutput, calls=%fused_computation.13 | convolution fusion | flops 135528448 | bytes 5373956 | tf_op jit(solution)/shard_map/while/body/eval_jaxpr/cond/branch_1_fun/dot_general | solution.py:32
  91.6 1.9 %subtract_convert_fusion.25 = (bf16[256,256]{1,0:T(8,128)(2,1)}, bf16[256,256]{1,0:T(8,128)(2,1)}, bf16[256,256]{1,0:T(8,128)(2,1)S(1)}, bf16[256,256]{1,0:T(8,128)(2,1)}) fusion(s32[256]{0:T(256)S(1)} %get-tuple-element.688), kind=kLoop, calls=%fused_computation.62.clone.1 | loop fusion | flops 1441792 | bytes 525312 | tf_op jit(solution)/shard_map/convert_element_type | solution.py:9
  95.9 13.5 %conditional.5 = ((f32[256,1024]{0,1:T(8,128)}, f32[256,1024]{0,1:T(8,128)}, f32[640,1024]{0,1:T(8,128)})) conditional(s32[]{:T(128)} %convert_element_type.670, (f32[256,1024]{0,1:T(8,128)}, f32[256,1024]{0,1:T(8,128)}, f32[640,1024]{0,1:T(8,128)}) %tuple.73, (s32[]{:T(128)}, bf16[4,128,1024]{2,1,0:T(8,128)(2,1)}, bf16[256,128]{1,0:T(8,128)(2,1)}, ...), branch_computations={%region_1.1_spmd, %region_2.2_spmd} | conditional | flops 1083179008 | bytes 39321852 | solution.py:111
  99.7 5.0 %multiply_subtract_fusion = (f32[256,1024]{0,1:T(8,128)S(1)}, f32[256,1024]{0,1:T(8,128)S(1)}, f32[256,1024]{0,1:T(8,128)}, f32[256,1024]{0,1:T(8,128)}) fusion(f32[256,1024]{0,1:T(8,128)} %get-tuple-element.336, f32[256,1024]{0,1:T(8,128)S(1)} %fusion.22, f32[256,1024]{0,1:T(8,128)} %get-tuple-element.335, f32[256,1024]{0,1:T(8,128)} %get-tuple-element.323, ...), kind=kOutput, calls=%fused_computation.31 | convolution fusion | flops 71041024 | bytes 12910600 | tf_op jit(solution)/shard_map/while/body/eval_jaxpr/cond/branch_1_fun/dot_general | solution.py:22
  106.6 2.7 %fusion.20 = f32[640,1024]{0,1:T(8,128)} fusion(f32[640,1024]{0,1:T(8,128)} %get-tuple-element.334, s32[]{:T(128)S(6)} %select_n.24, f32[1024,256]{1,0:T(8,128)S(1)} %convolution_add_fusion.2, f32[1024,256]{1,0:T(8,128)S(1)} %convolution_add_fusion.1, bf16[256,256]{1,0:T(8,128)(2,1)S(1)} %copy-done.2, f32[256,1024]{0,1:T(8,128)S(1)} %get-tuple-element.545), kind=kOutput, calls=%fused_computation.13 | convolution fusion | flops 135528448 | bytes 5373956 | tf_op jit(solution)/shard_map/while/body/eval_jaxpr/cond/branch_1_fun/dot_general | solution.py:32
  109.3 1.9 %subtract_convert_fusion.25 = (bf16[256,256]{1,0:T(8,128)(2,1)}, bf16[256,256]{1,0:T(8,128)(2,1)}, bf16[256,256]{1,0:T(8,128)(2,1)S(1)}, bf16[256,256]{1,0:T(8,128)(2,1)}) fusion(s32[256]{0:T(256)S(1)} %get-tuple-element.688), kind=kLoop, calls=%fused_computation.62.clone.1 | loop fusion | flops 1441792 | bytes 525312 | tf_op jit(solution)/shard_map/convert_element_type | solution.py:9
  113.6 13.4 %conditional.5 = ((f32[256,1024]{0,1:T(8,128)}, f32[256,1024]{0,1:T(8,128)}, f32[640,1024]{0,1:T(8,128)})) conditional(s32[]{:T(128)} %convert_element_type.670, (f32[256,1024]{0,1:T(8,128)}, f32[256,1024]{0,1:T(8,128)}, f32[640,1024]{0,1:T(8,128)}) %tuple.73, (s32[]{:T(128)}, bf16[4,128,1024]{2,1,0:T(8,128)(2,1)}, bf16[256,128]{1,0:T(8,128)(2,1)}, ...), branch_computations={%region_1.1_spmd, %region_2.2_spmd} | conditional | flops 1083179008 | bytes 39321852 | solution.py:111
  117.4 5.0 %multiply_subtract_fusion = (f32[256,1024]{0,1:T(8,128)S(1)}, f32[256,1024]{0,1:T(8,128)S(1)}, f32[256,1024]{0,1:T(8,128)}, f32[256,1024]{0,1:T(8,128)}) fusion(f32[256,1024]{0,1:T(8,128)} %get-tuple-element.336, f32[256,1024]{0,1:T(8,128)S(1)} %fusion.22, f32[256,1024]{0,1:T(8,128)} %get-tuple-element.335, f32[256,1024]{0,1:T(8,128)} %get-tuple-element.323, ...), kind=kOutput, calls=%fused_computation.31 | convolution fusion | flops 71041024 | bytes 12910600 | tf_op jit(solution)/shard_map/while/body/eval_jaxpr/cond/branch_1_fun/dot_general | solution.py:22
  124.4 2.6 %fusion.20 = f32[640,1024]{0,1:T(8,128)} fusion(f32[640,1024]{0,1:T(8,128)} %get-tuple-element.334, s32[]{:T(128)S(6)} %select_n.24, f32[1024,256]{1,0:T(8,128)S(1)} %convolution_add_fusion.2, f32[1024,256]{1,0:T(8,128)S(1)} %convolution_add_fusion.1, bf16[256,256]{1,0:T(8,128)(2,1)S(1)} %copy-done.2, f32[256,1024]{0,1:T(8,128)S(1)} %get-tuple-element.545), kind=kOutput, calls=%fused_computation.13 | convolution fusion | flops 135528448 | bytes 5373956 | tf_op jit(solution)/shard_map/while/body/eval_jaxpr/cond/branch_1_fun/dot_general | solution.py:32
  127.0 1.9 %subtract_convert_fusion.25 = (bf16[256,256]{1,0:T(8,128)(2,1)}, bf16[256,256]{1,0:T(8,128)(2,1)}, bf16[256,256]{1,0:T(8,128)(2,1)S(1)}, bf16[256,256]{1,0:T(8,128)(2,1)}) fusion(s32[256]{0:T(256)S(1)} %get-tuple-element.688), kind=kLoop, calls=%fused_computation.62.clone.1 | loop fusion | flops 1441792 | bytes 525312 | tf_op jit(solution)/shard_map/convert_element_type | solution.py:9
  131.2 13.4 %conditional.5 = ((f32[256,1024]{0,1:T(8,128)}, f32[256,1024]{0,1:T(8,128)}, f32[640,1024]{0,1:T(8,128)})) conditional(s32[]{:T(128)} %convert_element_type.670, (f32[256,1024]{0,1:T(8,128)}, f32[256,1024]{0,1:T(8,128)}, f32[640,1024]{0,1:T(8,128)}) %tuple.73, (s32[]{:T(128)}, bf16[4,128,1024]{2,1,0:T(8,128)(2,1)}, bf16[256,128]{1,0:T(8,128)(2,1)}, ...), branch_computations={%region_1.1_spmd, %region_2.2_spmd} | conditional | flops 1083179008 | bytes 39321852 | solution.py:111
  135.1 5.0 %multiply_subtract_fusion = (f32[256,1024]{0,1:T(8,128)S(1)}, f32[256,1024]{0,1:T(8,128)S(1)}, f32[256,1024]{0,1:T(8,128)}, f32[256,1024]{0,1:T(8,128)}) fusion(f32[256,1024]{0,1:T(8,128)} %get-tuple-element.336, f32[256,1024]{0,1:T(8,128)S(1)} %fusion.22, f32[256,1024]{0,1:T(8,128)} %get-tuple-element.335, f32[256,1024]{0,1:T(8,128)} %get-tuple-element.323, ...), kind=kOutput, calls=%fused_computation.31 | convolution fusion | flops 71041024 | bytes 12910600 | tf_op jit(solution)/shard_map/while/body/eval_jaxpr/cond/branch_1_fun/dot_general | solution.py:22
  142.0 2.6 %fusion.20 = f32[640,1024]{0,1:T(8,128)} fusion(f32[640,1024]{0,1:T(8,128)} %get-tuple-element.334, s32[]{:T(128)S(6)} %select_n.24, f32[1024,256]{1,0:T(8,128)S(1)} %convolution_add_fusion.2, f32[1024,256]{1,0:T(8,128)S(1)} %convolution_add_fusion.1, bf16[256,256]{1,0:T(8,128)(2,1)S(1)} %copy-done.2, f32[256,1024]{0,1:T(8,128)S(1)} %get-tuple-element.545), kind=kOutput, calls=%fused_computation.13 | convolution fusion | flops 135528448 | bytes 5373956 | tf_op jit(solution)/shard_map/while/body/eval_jaxpr/cond/branch_1_fun/dot_general | solution.py:32
  144.7 2.0 %copy.14 = bf16[640,1024]{1,0:T(8,128)(2,1)S(1)} copy(f32[640,1024]{0,1:T(8,128)} %get-tuple-element.374) | data formatting | bytes 3932160 | tf_op jit(solution)/shard_map/while | solution.py:113
  147.7 2.0 %fusion.131 = f32[128,1024]{1,0:T(8,128)S(1)} fusion(s32[128]{0:T(128)S(1)} %iota_add_fusion.1, f32[256,1024]{0,1:T(8,128)} %get-tuple-element.373), kind=kOutput, calls=%fused_computation.158 | convolution fusion | flops 67862528 | bytes 1573376 | tf_op jit(solution)/shard_map/dot_general | solution.py:30
  149.7 2.0 %fusion.135 = f32[128,1024]{1,0:T(8,128)S(1)} fusion(s32[128]{0:T(128)S(1)} %iota_add_fusion.1, f32[256,1024]{0,1:T(8,128)} %get-tuple-element.372), kind=kOutput, calls=%fused_computation.159 | convolution fusion | flops 67862528 | bytes 1573376 | tf_op jit(solution)/shard_map/dot_general | solution.py:30
  151.7 2.3 %convolution_add_fusion.9 = f32[128,1024]{1,0:T(8,128)S(1)} fusion(f32[128,1024]{1,0:T(8,128)S(1)} %fusion.131, f32[256,1024]{0,1:T(8,128)} %get-tuple-element.373, s32[128]{0:T(128)S(1)} %iota_add_fusion.1), kind=kOutput, calls=%fused_computation.98 | convolution fusion | flops 68780032 | bytes 2097664 | tf_op jit(solution)/shard_map/dot_general | solution.py:31
  154.0 2.3 %convolution_add_fusion.11 = f32[128,1024]{1,0:T(8,128)S(1)} fusion(f32[128,1024]{1,0:T(8,128)S(1)} %fusion.135, f32[256,1024]{0,1:T(8,128)} %get-tuple-element.372, s32[128]{0:T(128)S(1)} %iota_add_fusion.1), kind=kOutput, calls=%fused_computation.100 | convolution fusion | flops 68780032 | bytes 2097664 | tf_op jit(solution)/shard_map/dot_general | solution.py:31
  156.3 2.0 %convolution_add_fusion.10 = f32[128,1024]{1,0:T(8,128)S(1)} fusion(f32[128,1024]{1,0:T(8,128)S(1)} %convolution_add_fusion.11, s32[128]{0:T(128)S(1)} %iota_add_fusion.1, f32[256,1024]{0,1:T(8,128)} %get-tuple-element.372), kind=kOutput, calls=%fused_computation.99 | convolution fusion | flops 68091904 | bytes 2097664 | tf_op jit(solution)/shard_map/dot_general | solution.py:32
  158.3 2.7 %fusion.74 = bf16[128,1024]{1,0:T(8,128)(2,1)} fusion(f32[128,1024]{1,0:T(8,128)S(1)} %convolution_add_fusion.10, f32[128,1024]{1,0:T(8,128)S(1)} %convolution_add_fusion.9, bf16[128,1024]{1,0:T(8,128)(2,1)S(1)} %copy-done.5, f32[1024]{0:T(1024)S(1)} %copy-done.6, s32[128]{0:T(128)S(1)} %iota_add_fusion.1, f32[256,1024]{0,1:T(8,128)} %get-tuple-element.373), kind=kOutput, calls=%fused_computation.101 | convolution fusion | flops 68878336 | bytes 2626048 | tf_op jit(solution)/shard_map/dot_general | solution.py:32
  161.0 12.1 %reduce-scatter.2.cloned.1.call-done = bf16[128,1024]{1,0:T(8,128)(2,1)} async-done(((bf16[512,1024]{1,0:T(8,128)(2,1)}), bf16[128,1024]{1,0:T(8,128)(2,1)}) %reduce-scatter.2.cloned.1.call-update) | async-done | bytes 262160 | tf_op jit(solution)/shard_map/reduce_scatter | solution.py:118
  173.2 1.8 convert_element_type.265
  (94 shorter events, 47.9 us)
Async XLA Ops:
  7.2 2.7 %copy-start = (bf16[128,1024]{1,0:T(8,128)(2,1)S(1)}, bf16[128,1024]{1,0:T(8,128)(2,1)}, u32[]{:S(2)}) copy-start(bf16[128,1024]{1,0:T(8,128)(2,1)} %param.11) | copy-start | bytes 786436
  7.2 33.1 %all-gather.4.cloned.1.call-start = ((), (), s32[]{:S(2)}) async-start(), calls=%async_computation.1 | async-start | bytes 1310720 | tf_op jit(solution)/shard_map/all_gather | solution.py:72
  7.9 62.1 %all-gather.6.cloned.1.call-start = ((), (), s32[]{:S(2)}) async-start(), calls=%async_computation.3 | async-start | bytes 1310720 | tf_op jit(solution)/shard_map/all_gather | solution.py:99
  9.8 163.4 %reduce-scatter.2.cloned.1.call-start = ((), (), s32[]{:S(2)}) async-start(), calls=%async_computation.2 | async-start | bytes 1310720 | tf_op jit(solution)/shard_map/reduce_scatter | solution.py:118
  40.2 2.2 %copy-start.4 = (bf16[512,1024]{1,0:T(8,128)(2,1)S(1)}, bf16[512,1024]{1,0:T(8,128)(2,1)}, u32[]{:S(2)}) copy-start(bf16[512,1024]{1,0:T(8,128)(2,1)} %all-gather.4.cloned.1.call-done) | copy-start | bytes 3145732
  87.0 0.9 copy-start.1
  87.3 1.3 copy-start.3
  87.9 1.0 copy-start.2
  104.7 0.9 copy-start.1
  105.0 1.2 copy-start.3
  105.6 1.0 copy-start.2
  122.4 0.9 copy-start.1
  122.8 1.2 copy-start.3
  123.3 1.0 copy-start.2
  140.1 0.9 copy-start.1
  140.4 1.3 copy-start.3
  141.0 1.0 copy-start.2
  149.7 8.6 %copy-start.5 = (bf16[128,1024]{1,0:T(8,128)(2,1)S(1)}, bf16[128,1024]{1,0:T(8,128)(2,1)}, u32[]{:S(2)}) copy-start(bf16[128,1024]{1,0:T(8,128)(2,1)} %multiply_convert_fusion) | copy-start | bytes 786436
  149.7 8.6 %copy-start.6 = (f32[1024]{0:T(1024)S(1)}, f32[1024]{0:T(1024)}, u32[]{:S(2)}) copy-start(f32[1024]{0:T(1024)} %param.13) | copy-start | bytes 12292
Sparse Core Ops, SparseCore 0:
  9.6 30.6 all-gather.3
  42.4 27.5 all-gather.5
  147.8 25.2 reduce-scatter.1
where the time goes:
time: 182 us; the launch traced here: 181 us
  matrix products  79.1 us (43%)
  waiting for transfers between devices  54 us (30%)
  other arithmetic  20.7 us (11%)
  between operations  13.9 us (8%)
  local copies, waits for them, and re-layouts  13.3 us (7%)
    dot_general x10, matrix products, table_times(): jnp.dot(low_part, signal, preferred_element_type=jnp.float32)  26.5 us
    all_gather x1, waiting for transfers between devices, shards(): taps = lax.all_gather(filter_taps, 'ctx', axis=0, tiled=True)  24.8 us
    dot_general x10, matrix products, table_times_float(): jnp.dot(low_part, value_high, preferred_element_type=jnp.float32)  16.6 us
    all_gather x1, waiting for transfers between devices, shards(): spans = lax.all_gather(grad_y[None], 'ctx', axis=0, tiled=True)  16.3 us
    convert_element_type x8, other arithmetic, split_parts(): low_part = (values - high_part.astype(jnp.float32)).astype(jnp.bfloat16)  12.4 us
    reduce_scatter x1, waiting for transfers between devices, shards(): lax.psum_scatter(lag_sums[span_len:].astype(jnp.bfloat16), 'ctx', scatter...  12.1 us
    dot_general x10, matrix products, table_times(): jnp.dot(high_part, signal, preferred_element_type=jnp.float32)  11.6 us
    dot_general x10, matrix products, table_times_float(): jnp.dot(high_part, value_low, preferred_element_type=jnp.float32)  7.3 us
  transfers between devices with their start and end apart: 3, of which 3 were waited for; matrix products, arithmetic and copies ran while one was open for 19% of the time, Pallas kernels for 0%

commit v1 on v0

--- a/solution.py
+++ b/solution.py
@@ -2,6 +2,30 @@
 import jax.numpy as jnp
 from jax import lax
 from jax.sharding import PartitionSpec as P
+
+
+def close_links_on_mesh(point, chip_axis):
+    r2, field_out, item_now = (lax.psum(1, chip_axis), lax.axis_index(chip_axis), point.shape[0])
+    block_list = [u * r2 if dev_i == 0 else u for dev_i, u in enumerate(point.shape)]
+    answer = aux = point
+    carry_in = lax.dynamic_update_slice_in_dim(
+        jnp.zeros(block_list, point.dtype), point, field_out * item_now, axis=0
+    )
+    for ix in range(1, r2 // 2 + 1):
+        answer = lax.ppermute(
+            answer, chip_axis, list(map(lambda dev_i: (dev_i, (dev_i + 1) % r2), range(r2)))
+        )
+        carry_in = lax.dynamic_update_slice_in_dim(
+            carry_in, answer, (field_out - ix) % r2 * item_now, axis=0
+        )
+        if 2 * ix < r2:
+            aux = lax.ppermute(
+                aux, chip_axis, list(map(lambda dev_i: (dev_i, (dev_i - 1) % r2), range(r2)))
+            )
+            carry_in = lax.dynamic_update_slice_in_dim(
+                carry_in, aux, (field_out + ix) % r2 * item_now, axis=0
+            )
+    return carry_in
 
 
 def split_parts(values):
@@ -69,7 +93,7 @@
     full_fwd = phase_tables(period, period, 0, period)
     short_inv = phase_tables(span_len, period, span_len, period)
     full_inv = phase_tables(period, period, span_len, period)
-    taps = lax.all_gather(filter_taps, "ctx", axis=0, tiled=True)
+    taps = close_links_on_mesh(filter_taps, chip_axis="ctx")
     taps_padded = jnp.concatenate([jnp.zeros((span_len, channels), jnp.bfloat16), taps], axis=0)
     windows = jnp.concatenate(
         [

time: 182 us -> 162 us (0.89)
  waiting for transfers between devices: 54 us -> 23.4 us
  starting transfers between devices: 0.12 us -> 5.31 us
  local copies, waits for them, and re-layouts: 13.3 us -> 16.2 us
  matrix products: 79.1 us -> 81 us
    all_gather x1 -> x0, waiting for transfers between devices: 24.8 us -> none  [shards(): taps = lax.all_gather(filter_taps, 'ctx', axis=0, tiled=True)]
    all_gather x1, waiting for transfers between devices: 16.3 us -> 0.01 us  [shards(): spans = lax.all_gather(grad_y[None], 'ctx', axis=0, tiled=True)]
    ppermute x0 -> x3, waiting for transfers between devices: none -> 11.2 us  [the longest x2 11.2 us: close_links_on_mesh(): lax.ppermute(answer, chip_axis, list(map(lambda dev_i: (dev_i, (dev_i + 1...]
    ppermute x0 -> x3, starting transfers between devices: none -> 5.23 us  [the longest x2 3.14 us: close_links_on_mesh(): lax.ppermute(answer, chip_axis, list(map(lambda dev_i: (dev_i, (dev_i + 1...]
    dynamic_update_slice x0 -> x4, local copies, waits for them, and re-layouts: none -> 3.96 us  [the longest x2 1.94 us: close_links_on_mesh(): lax.dynamic_update_slice_in_dim(carry_in, answer, (field_out - ix) % r2 *...]
    dot_general x10, matrix products: 26.5 us -> 28.5 us  [table_times(): jnp.dot(low_part, signal, preferred_element_type=jnp.float32)]
  transfers between devices with their start and end apart: 3 -> 5, of which waited for: 3 -> 2; matrix products, arithmetic and copies ran while one was open for 19% -> 24% of each run, Pallas kernels for 0% -> 0%
where the time goes in v1:
time: 162 us; the launch traced here: 161 us
  matrix products  81 us (50%)
  waiting for transfers between devices  23.4 us (14%)
  other arithmetic  20.7 us (13%)
  local copies, waits for them, and re-layouts  16.2 us (10%)
  between operations  14.3 us (9%)
  starting transfers between devices  5.31 us (3%)
    dot_general x10, matrix products, table_times(): jnp.dot(low_part, signal, preferred_element_type=jnp.float32)  28.5 us
    dot_general x10, matrix products, table_times_float(): jnp.dot(low_part, value_high, preferred_element_type=jnp.float32)  16.5 us
    convert_element_type x8, other arithmetic, split_parts(): low_part = (values - high_part.astype(jnp.float32)).astype(jnp.bfloat16)  12.4 us
    reduce_scatter x1, waiting for transfers between devices, shards(): lax.psum_scatter(lag_sums[span_len:].astype(jnp.bfloat16), 'ctx', scatter...  12.3 us
    dot_general x10, matrix products, table_times(): jnp.dot(high_part, signal, preferred_element_type=jnp.float32)  11.6 us
    ppermute x2, waiting for transfers between devices, close_links_on_mesh(): lax.ppermute(answer, chip_axis, list(map(lambda dev_i: (dev_i, (dev_i + 1...  11.2 us
    dot_general x10, matrix products, table_times_float(): jnp.dot(high_part, value_low, preferred_element_type=jnp.float32)  7.3 us
    dot_general x2, matrix products, batched_times(): jnp.einsum('pr,nrc->npc', low_part, blocks, preferred_element_type=jnp.fl...  7.28 us
  transfers between devices with their start and end apart: 5, of which 2 were waited for; matrix products, arithmetic and copies ran while one was open for 24% of the time, Pallas kernels for 0%

profile of v1, /device:TPU:0, one launch (start us, length us, event | category | flops | bytes accessed | tf_op | source)
XLA Modules:
  0.0 161.4 jit_solution(13340014230642030902)
XLA Ops:
  7.2 3.1 %collective-permute-start = (bf16[128,1024]{1,0:T(8,128)(2,1)}, bf16[128,1024]{1,0:T(8,128)(2,1)}, u32[]{:S(2)}, u32[]{:S(2)}) collective-permute-start(bf16[128,1024]{1,0:T(8,128)(2,1)} %param.12), channel_id=1, source_target_pairs={{0,4},{4,8},{8,12},{12,0},{1,5},{5,9},{9,13},{13,1},{2,6},{6,10},{... | collective-permute-start | bytes 786440 | tf_op jit(solution)/shard_map/ppermute | solution.py:15
  10.3 2.1 %collective-permute-start.1 = (bf16[128,1024]{1,0:T(8,128)(2,1)}, bf16[128,1024]{1,0:T(8,128)(2,1)}, u32[]{:S(2)}, u32[]{:S(2)}) collective-permute-start(bf16[128,1024]{1,0:T(8,128)(2,1)} %param.12), channel_id=1, source_target_pairs={{0,12},{4,0},{8,4},{12,8},{1,13},{5,1},{9,5},{13,9},{2,14},{6,2},{... | collective-permute-start | bytes 786440 | tf_op jit(solution)/shard_map/ppermute | solution.py:22
  12.4 1.8 %multiply_convert_fusion = bf16[128,1024]{1,0:T(8,128)(2,1)} fusion(bf16[128,1024]{1,0:T(8,128)(2,1)} %param.10, bf16[128,1024]{1,0:T(8,128)(2,1)} %param.9), kind=kLoop, calls=%fused_computation.104 | loop fusion | flops 524288 | bytes 786432 | tf_op jit(solution)/shard_map/convert_element_type | solution.py:91
  25.1 11.1 %collective-permute-done.2 = bf16[128,1024]{1,0:T(8,128)(2,1)} collective-permute-done((bf16[128,1024]{1,0:T(8,128)(2,1)}, bf16[128,1024]{1,0:T(8,128)(2,1)}, u32[]{:S(2)}, u32[]{:S(2)}) %collective-permute-start.2) | collective-permute-done | bytes 262176 | tf_op jit(solution)/shard_map/ppermute | solution.py:15
  42.2 3.7 %negate_bitcast_fusion = f32[4,256,1024]{1,2,0:T(8,128)} fusion(f32[4,1024,256]{2,1,0:T(8,128)S(1)} %fusion.91, bf16[4,128,1024]{1,2,0:T(8,128)(2,1)S(1)} %copy.11, bf16[4,128,1024]{1,2,0:T(8,128)(2,1)S(1)} %copy.10), kind=kOutput, calls=%fused_computation.86 | convolution fusion | flops 544342016 | bytes 10485760 | tf_op jit(solution)/shard_map/pr,nrc->npc/dot_general | solution.py:75
  45.9 3.6 %add_bitcast_fusion = f32[4,256,1024]{1,2,0:T(8,128)} fusion(f32[4,1024,256]{2,1,0:T(8,128)S(1)} %fusion.93, bf16[4,128,1024]{1,2,0:T(8,128)(2,1)S(1)} %copy.11, bf16[4,128,1024]{1,2,0:T(8,128)(2,1)S(1)} %copy.10), kind=kOutput, calls=%fused_computation.87 | convolution fusion | flops 543293440 | bytes 10485760 | tf_op jit(solution)/shard_map/pr,nrc->npc/dot_general | solution.py:75
  53.3 70.8 %while.20 = (s32[]{:T(128)}, f32[256,1024]{0,1:T(8,128)}, f32[256,1024]{0,1:T(8,128)}, f32[640,1024]{0,1:T(8,128)}, s32[]{:T(128)}, /*index=5*/bf16[4,128,1024]{...) while((s32[]{:T(128)}, f32[256,1024]{0,1:T(8,128)}, ...), condition=%wide.region_3.4_spmd.clone.clone.clone, body=%wide.region_0.3_spmd.clone.clone.clone.sunk | while | flops 1085865984 | bytes 40109640 | solution.py:137
  53.3 1.9 %subtract_convert_fusion.25 = (bf16[256,256]{1,0:T(8,128)(2,1)}, bf16[256,256]{1,0:T(8,128)(2,1)}, bf16[256,256]{1,0:T(8,128)(2,1)S(1)}, bf16[256,256]{1,0:T(8,128)(2,1)}) fusion(s32[256]{0:T(256)S(1)} %get-tuple-element.688), kind=kLoop, calls=%fused_computation.62.clone.1 | loop fusion | flops 1441792 | bytes 525312 | tf_op jit(solution)/shard_map/convert_element_type | solution.py:33
  57.6 13.4 %conditional.5 = ((f32[256,1024]{0,1:T(8,128)}, f32[256,1024]{0,1:T(8,128)}, f32[640,1024]{0,1:T(8,128)})) conditional(s32[]{:T(128)} %convert_element_type.670, (f32[256,1024]{0,1:T(8,128)}, f32[256,1024]{0,1:T(8,128)}, f32[640,1024]{0,1:T(8,128)}) %tuple.73, (s32[]{:T(128)}, bf16[4,128,1024]{2,1,0:T(8,128)(2,1)}, bf16[256,128]{1,0:T(8,128)(2,1)}, ...), branch_computations={%region_1.1_spmd, %region_2.2_spmd} | conditional | flops 1083179008 | bytes 39321852 | solution.py:135
  61.4 5.0 %multiply_subtract_fusion = (f32[256,1024]{0,1:T(8,128)S(1)}, f32[256,1024]{0,1:T(8,128)S(1)}, f32[256,1024]{0,1:T(8,128)}, f32[256,1024]{0,1:T(8,128)}) fusion(f32[256,1024]{0,1:T(8,128)} %get-tuple-element.336, f32[256,1024]{0,1:T(8,128)S(1)} %fusion.22, f32[256,1024]{0,1:T(8,128)} %get-tuple-element.335, f32[256,1024]{0,1:T(8,128)} %get-tuple-element.323, ...), kind=kOutput, calls=%fused_computation.31 | convolution fusion | flops 71041024 | bytes 12910600 | tf_op jit(solution)/shard_map/while/body/eval_jaxpr/cond/branch_1_fun/dot_general | solution.py:46
  68.4 2.6 %fusion.20 = f32[640,1024]{0,1:T(8,128)} fusion(f32[640,1024]{0,1:T(8,128)} %get-tuple-element.334, s32[]{:T(128)S(6)} %select_n.70, f32[1024,256]{1,0:T(8,128)S(1)} %convolution_add_fusion.2, f32[1024,256]{1,0:T(8,128)S(1)} %convolution_add_fusion.1, bf16[256,256]{1,0:T(8,128)(2,1)S(1)} %copy-done.2, f32[256,1024]{0,1:T(8,128)S(1)} %get-tuple-element.545), kind=kOutput, calls=%fused_computation.13 | convolution fusion | flops 135528448 | bytes 5373956 | tf_op jit(solution)/shard_map/while/body/eval_jaxpr/cond/branch_1_fun/dot_general | solution.py:56
  71.0 1.9 %subtract_convert_fusion.25 = (bf16[256,256]{1,0:T(8,128)(2,1)}, bf16[256,256]{1,0:T(8,128)(2,1)}, bf16[256,256]{1,0:T(8,128)(2,1)S(1)}, bf16[256,256]{1,0:T(8,128)(2,1)}) fusion(s32[256]{0:T(256)S(1)} %get-tuple-element.688), kind=kLoop, calls=%fused_computation.62.clone.1 | loop fusion | flops 1441792 | bytes 525312 | tf_op jit(solution)/shard_map/convert_element_type | solution.py:33
  75.3 13.4 %conditional.5 = ((f32[256,1024]{0,1:T(8,128)}, f32[256,1024]{0,1:T(8,128)}, f32[640,1024]{0,1:T(8,128)})) conditional(s32[]{:T(128)} %convert_element_type.670, (f32[256,1024]{0,1:T(8,128)}, f32[256,1024]{0,1:T(8,128)}, f32[640,1024]{0,1:T(8,128)}) %tuple.73, (s32[]{:T(128)}, bf16[4,128,1024]{2,1,0:T(8,128)(2,1)}, bf16[256,128]{1,0:T(8,128)(2,1)}, ...), branch_computations={%region_1.1_spmd, %region_2.2_spmd} | conditional | flops 1083179008 | bytes 39321852 | solution.py:135
  79.1 5.0 %multiply_subtract_fusion = (f32[256,1024]{0,1:T(8,128)S(1)}, f32[256,1024]{0,1:T(8,128)S(1)}, f32[256,1024]{0,1:T(8,128)}, f32[256,1024]{0,1:T(8,128)}) fusion(f32[256,1024]{0,1:T(8,128)} %get-tuple-element.336, f32[256,1024]{0,1:T(8,128)S(1)} %fusion.22, f32[256,1024]{0,1:T(8,128)} %get-tuple-element.335, f32[256,1024]{0,1:T(8,128)} %get-tuple-element.323, ...), kind=kOutput, calls=%fused_computation.31 | convolution fusion | flops 71041024 | bytes 12910600 | tf_op jit(solution)/shard_map/while/body/eval_jaxpr/cond/branch_1_fun/dot_general | solution.py:46
  86.0 2.6 %fusion.20 = f32[640,1024]{0,1:T(8,128)} fusion(f32[640,1024]{0,1:T(8,128)} %get-tuple-element.334, s32[]{:T(128)S(6)} %select_n.70, f32[1024,256]{1,0:T(8,128)S(1)} %convolution_add_fusion.2, f32[1024,256]{1,0:T(8,128)S(1)} %convolution_add_fusion.1, bf16[256,256]{1,0:T(8,128)(2,1)S(1)} %copy-done.2, f32[256,1024]{0,1:T(8,128)S(1)} %get-tuple-element.545), kind=kOutput, calls=%fused_computation.13 | convolution fusion | flops 135528448 | bytes 5373956 | tf_op jit(solution)/shard_map/while/body/eval_jaxpr/cond/branch_1_fun/dot_general | solution.py:56
  88.7 1.9 %subtract_convert_fusion.25 = (bf16[256,256]{1,0:T(8,128)(2,1)}, bf16[256,256]{1,0:T(8,128)(2,1)}, bf16[256,256]{1,0:T(8,128)(2,1)S(1)}, bf16[256,256]{1,0:T(8,128)(2,1)}) fusion(s32[256]{0:T(256)S(1)} %get-tuple-element.688), kind=kLoop, calls=%fused_computation.62.clone.1 | loop fusion | flops 1441792 | bytes 525312 | tf_op jit(solution)/shard_map/convert_element_type | solution.py:33
  93.0 13.4 %conditional.5 = ((f32[256,1024]{0,1:T(8,128)}, f32[256,1024]{0,1:T(8,128)}, f32[640,1024]{0,1:T(8,128)})) conditional(s32[]{:T(128)} %convert_element_type.670, (f32[256,1024]{0,1:T(8,128)}, f32[256,1024]{0,1:T(8,128)}, f32[640,1024]{0,1:T(8,128)}) %tuple.73, (s32[]{:T(128)}, bf16[4,128,1024]{2,1,0:T(8,128)(2,1)}, bf16[256,128]{1,0:T(8,128)(2,1)}, ...), branch_computations={%region_1.1_spmd, %region_2.2_spmd} | conditional | flops 1083179008 | bytes 39321852 | solution.py:135
  96.8 5.0 %multiply_subtract_fusion = (f32[256,1024]{0,1:T(8,128)S(1)}, f32[256,1024]{0,1:T(8,128)S(1)}, f32[256,1024]{0,1:T(8,128)}, f32[256,1024]{0,1:T(8,128)}) fusion(f32[256,1024]{0,1:T(8,128)} %get-tuple-element.336, f32[256,1024]{0,1:T(8,128)S(1)} %fusion.22, f32[256,1024]{0,1:T(8,128)} %get-tuple-element.335, f32[256,1024]{0,1:T(8,128)} %get-tuple-element.323, ...), kind=kOutput, calls=%fused_computation.31 | convolution fusion | flops 71041024 | bytes 12910600 | tf_op jit(solution)/shard_map/while/body/eval_jaxpr/cond/branch_1_fun/dot_general | solution.py:46
  103.8 2.7 %fusion.20 = f32[640,1024]{0,1:T(8,128)} fusion(f32[640,1024]{0,1:T(8,128)} %get-tuple-element.334, s32[]{:T(128)S(6)} %select_n.70, f32[1024,256]{1,0:T(8,128)S(1)} %convolution_add_fusion.2, f32[1024,256]{1,0:T(8,128)S(1)} %convolution_add_fusion.1, bf16[256,256]{1,0:T(8,128)(2,1)S(1)} %copy-done.2, f32[256,1024]{0,1:T(8,128)S(1)} %get-tuple-element.545), kind=kOutput, calls=%fused_computation.13 | convolution fusion | flops 135528448 | bytes 5373956 | tf_op jit(solution)/shard_map/while/body/eval_jaxpr/cond/branch_1_fun/dot_general | solution.py:56
  106.4 1.9 %subtract_convert_fusion.25 = (bf16[256,256]{1,0:T(8,128)(2,1)}, bf16[256,256]{1,0:T(8,128)(2,1)}, bf16[256,256]{1,0:T(8,128)(2,1)S(1)}, bf16[256,256]{1,0:T(8,128)(2,1)}) fusion(s32[256]{0:T(256)S(1)} %get-tuple-element.688), kind=kLoop, calls=%fused_computation.62.clone.1 | loop fusion | flops 1441792 | bytes 525312 | tf_op jit(solution)/shard_map/convert_element_type | solution.py:33
  110.7 13.4 %conditional.5 = ((f32[256,1024]{0,1:T(8,128)}, f32[256,1024]{0,1:T(8,128)}, f32[640,1024]{0,1:T(8,128)})) conditional(s32[]{:T(128)} %convert_element_type.670, (f32[256,1024]{0,1:T(8,128)}, f32[256,1024]{0,1:T(8,128)}, f32[640,1024]{0,1:T(8,128)}) %tuple.73, (s32[]{:T(128)}, bf16[4,128,1024]{2,1,0:T(8,128)(2,1)}, bf16[256,128]{1,0:T(8,128)(2,1)}, ...), branch_computations={%region_1.1_spmd, %region_2.2_spmd} | conditional | flops 1083179008 | bytes 39321852 | solution.py:135
  114.6 5.0 %multiply_subtract_fusion = (f32[256,1024]{0,1:T(8,128)S(1)}, f32[256,1024]{0,1:T(8,128)S(1)}, f32[256,1024]{0,1:T(8,128)}, f32[256,1024]{0,1:T(8,128)}) fusion(f32[256,1024]{0,1:T(8,128)} %get-tuple-element.336, f32[256,1024]{0,1:T(8,128)S(1)} %fusion.22, f32[256,1024]{0,1:T(8,128)} %get-tuple-element.335, f32[256,1024]{0,1:T(8,128)} %get-tuple-element.323, ...), kind=kOutput, calls=%fused_computation.31 | convolution fusion | flops 71041024 | bytes 12910600 | tf_op jit(solution)/shard_map/while/body/eval_jaxpr/cond/branch_1_fun/dot_general | solution.py:46
  121.5 2.6 %fusion.20 = f32[640,1024]{0,1:T(8,128)} fusion(f32[640,1024]{0,1:T(8,128)} %get-tuple-element.334, s32[]{:T(128)S(6)} %select_n.70, f32[1024,256]{1,0:T(8,128)S(1)} %convolution_add_fusion.2, f32[1024,256]{1,0:T(8,128)S(1)} %convolution_add_fusion.1, bf16[256,256]{1,0:T(8,128)(2,1)S(1)} %copy-done.2, f32[256,1024]{0,1:T(8,128)S(1)} %get-tuple-element.545), kind=kOutput, calls=%fused_computation.13 | convolution fusion | flops 135528448 | bytes 5373956 | tf_op jit(solution)/shard_map/while/body/eval_jaxpr/cond/branch_1_fun/dot_general | solution.py:56
  124.1 2.0 %copy.14 = bf16[640,1024]{1,0:T(8,128)(2,1)S(1)} copy(f32[640,1024]{0,1:T(8,128)} %get-tuple-element.374) | data formatting | bytes 3932160 | tf_op jit(solution)/shard_map/while | solution.py:137
  127.2 2.0 %fusion.131 = f32[128,1024]{1,0:T(8,128)S(1)} fusion(s32[128]{0:T(128)S(1)} %iota_add_fusion.1, f32[256,1024]{0,1:T(8,128)} %get-tuple-element.373), kind=kOutput, calls=%fused_computation.158 | convolution fusion | flops 67862528 | bytes 1573376 | tf_op jit(solution)/shard_map/dot_general | solution.py:54
  129.1 2.0 %fusion.135 = f32[128,1024]{1,0:T(8,128)S(1)} fusion(s32[128]{0:T(128)S(1)} %iota_add_fusion.1, f32[256,1024]{0,1:T(8,128)} %get-tuple-element.372), kind=kOutput, calls=%fused_computation.159 | convolution fusion | flops 67862528 | bytes 1573376 | tf_op jit(solution)/shard_map/dot_general | solution.py:54
  131.1 2.3 %convolution_add_fusion.9 = f32[128,1024]{1,0:T(8,128)S(1)} fusion(f32[128,1024]{1,0:T(8,128)S(1)} %fusion.131, f32[256,1024]{0,1:T(8,128)} %get-tuple-element.373, s32[128]{0:T(128)S(1)} %iota_add_fusion.1), kind=kOutput, calls=%fused_computation.98 | convolution fusion | flops 68780032 | bytes 2097664 | tf_op jit(solution)/shard_map/dot_general | solution.py:55
  133.5 2.3 %convolution_add_fusion.11 = f32[128,1024]{1,0:T(8,128)S(1)} fusion(f32[128,1024]{1,0:T(8,128)S(1)} %fusion.135, f32[256,1024]{0,1:T(8,128)} %get-tuple-element.372, s32[128]{0:T(128)S(1)} %iota_add_fusion.1), kind=kOutput, calls=%fused_computation.100 | convolution fusion | flops 68780032 | bytes 2097664 | tf_op jit(solution)/shard_map/dot_general | solution.py:55
  135.8 2.0 %convolution_add_fusion.10 = f32[128,1024]{1,0:T(8,128)S(1)} fusion(f32[128,1024]{1,0:T(8,128)S(1)} %convolution_add_fusion.11, s32[128]{0:T(128)S(1)} %iota_add_fusion.1, f32[256,1024]{0,1:T(8,128)} %get-tuple-element.372), kind=kOutput, calls=%fused_computation.99 | convolution fusion | flops 68091904 | bytes 2097664 | tf_op jit(solution)/shard_map/dot_general | solution.py:56
  137.8 2.7 %fusion.74 = bf16[128,1024]{1,0:T(8,128)(2,1)} fusion(f32[128,1024]{1,0:T(8,128)S(1)} %convolution_add_fusion.10, f32[128,1024]{1,0:T(8,128)S(1)} %convolution_add_fusion.9, bf16[128,1024]{1,0:T(8,128)(2,1)S(1)} %copy-done.6, f32[1024]{0:T(1024)S(1)} %copy-done.7, s32[128]{0:T(128)S(1)} %iota_add_fusion.1, f32[256,1024]{0,1:T(8,128)} %get-tuple-element.373), kind=kOutput, calls=%fused_computation.101 | convolution fusion | flops 68878336 | bytes 2626048 | tf_op jit(solution)/shard_map/dot_general | solution.py:56
  140.5 12.3 %reduce-scatter.2.cloned.1.call-done = bf16[128,1024]{1,0:T(8,128)(2,1)} async-done(((bf16[512,1024]{1,0:T(8,128)(2,1)}), bf16[128,1024]{1,0:T(8,128)(2,1)}) %reduce-scatter.2.cloned.1.call-update) | async-done | bytes 262160 | tf_op jit(solution)/shard_map/reduce_scatter | solution.py:142
  152.7 1.8 %convert_element_type.265 = f32[128,1024]{1,0:T(8,128)} convert(bf16[128,1024]{1,0:T(8,128)(2,1)} %reduce-scatter.2.cloned.1.call-done) | non-fusion elementwise | flops 131072 | bytes 786432 | tf_op jit(solution)/shard_map/convert_element_type | solution.py:144
  (104 shorter events, 53.9 us)
Async XLA Ops:
  7.2 7.1 %copy-start = (bf16[128,1024]{1,0:T(8,128)(2,1)S(1)}, bf16[128,1024]{1,0:T(8,128)(2,1)}, u32[]{:S(2)}) copy-start(bf16[128,1024]{1,0:T(8,128)(2,1)} %param.11) | copy-start | bytes 786436
  7.2 42.3 %all-gather.3.cloned.1.call-start = ((), (), s32[]{:S(2)}) async-start(), calls=%async_computation.2 | async-start | bytes 1310720 | tf_op jit(solution)/shard_map/all_gather | solution.py:123
  7.2 13.1 %collective-permute-start = (bf16[128,1024]{1,0:T(8,128)(2,1)}, bf16[128,1024]{1,0:T(8,128)(2,1)}, u32[]{:S(2)}, u32[]{:S(2)}) collective-permute-start(bf16[128,1024]{1,0:T(8,128)(2,1)} %param.12), channel_id=1, source_target_pairs={{0,4},{4,8},{8,12},{12,0},{1,5},{5,9},{9,13},{13,1},{2,6},{6,10},{... | collective-permute-start | bytes 786440 | tf_op jit(solution)/shard_map/ppermute | solution.py:15
  10.3 13.8 %collective-permute-start.1 = (bf16[128,1024]{1,0:T(8,128)(2,1)}, bf16[128,1024]{1,0:T(8,128)(2,1)}, u32[]{:S(2)}, u32[]{:S(2)}) collective-permute-start(bf16[128,1024]{1,0:T(8,128)(2,1)} %param.12), channel_id=1, source_target_pairs={{0,12},{4,0},{8,4},{12,8},{1,13},{5,1},{9,5},{13,9},{2,14},{6,2},{... | collective-permute-start | bytes 786440 | tf_op jit(solution)/shard_map/ppermute | solution.py:22
  14.2 138.5 %reduce-scatter.2.cloned.1.call-start = ((), (), s32[]{:S(2)}) async-start(), calls=%async_computation.1 | async-start | bytes 1310720 | tf_op jit(solution)/shard_map/reduce_scatter | solution.py:142
  17.4 3.0 %copy-start.4 = (f32[256,1024]{1,0:T(8,128)S(1)}, f32[256,1024]{1,0:T(8,128)}, u32[]{:S(2)}) copy-start(f32[256,1024]{1,0:T(8,128)} %convolution_add_fusion.7) | copy-start | bytes 3145732
  19.1 2.7 %copy-start.5 = (f32[256,1024]{1,0:T(8,128)S(1)}, f32[256,1024]{1,0:T(8,128)}, u32[]{:S(2)}) copy-start(f32[256,1024]{1,0:T(8,128)} %fusion.70) | copy-start | bytes 3145732
  20.3 15.9 %collective-permute-start.2 = (bf16[128,1024]{1,0:T(8,128)(2,1)}, bf16[128,1024]{1,0:T(8,128)(2,1)}, u32[]{:S(2)}, u32[]{:S(2)}) collective-permute-start(bf16[128,1024]{1,0:T(8,128)(2,1)} %collective-permute-done), channel_id=1, source_target_pairs={{0,4},{4,8},{8,12},{12,0},{1,5},{5,9},{9,13},{13,1},{2,6},{6,10},{... | collective-permute-start | bytes 786440 | tf_op jit(solution)/shard_map/ppermute | solution.py:15
  66.4 0.9 copy-start.1
  66.8 1.3 copy-start.3
  67.3 1.0 copy-start.2
  84.1 0.9 copy-start.1
  84.4 1.2 copy-start.3
  85.0 1.0 copy-start.2
  101.8 0.9 copy-start.1
  102.2 1.2 copy-start.3
  102.7 1.0 copy-start.2
  119.5 0.9 copy-start.1
  119.9 1.2 copy-start.3
  120.5 1.0 copy-start.2
  129.1 8.6 %copy-start.6 = (bf16[128,1024]{1,0:T(8,128)(2,1)S(1)}, bf16[128,1024]{1,0:T(8,128)(2,1)}, u32[]{:S(2)}) copy-start(bf16[128,1024]{1,0:T(8,128)(2,1)} %multiply_convert_fusion) | copy-start | bytes 786436
  129.1 8.6 %copy-start.7 = (f32[1024]{0:T(1024)S(1)}, f32[1024]{0:T(1024)}, u32[]{:S(2)}) copy-start(f32[1024]{0:T(1024)} %param.13) | copy-start | bytes 12292
Sparse Core Ops, SparseCore 0:
  14.3 33.0 all-gather.2
  127.3 25.4 reduce-scatter.1
